TPU v7x, 512 devices: a whole 4x8x8 slice. The times are simulated.
512 devices in a mesh: ax: 64 (over z, y_hi, x), rad: 8 (over y_lo, core).
Axes of the slice: x: 4, y: 8 (y_hi: 2, y_lo: 4; y = y_hi * 4 + y_lo), z: 8, core: 2. Of those that a mesh axis runs over, the one named last changes fastest.
Arguments:
- parcel_motion: float32 [6, 1048576], P(None, ('ax', 'rad')), may hold values from -6 to 6
- parcel_size: float32 [1048576], P(('ax', 'rad')), may hold values from 0.5 to 2
- parcel_block: int32 [16384], P(('ax', 'rad')), may hold values from 0 to 511, as said below
- parcel_offset: int32 [1048576], P(('ax', 'rad')), may hold values from 0 to 127
- gas_velocity: float32 [3, 1024, 4096], P(None, 'ax', 'rad'), may hold values from -6 to 6
- pressure: float32 [1024, 4096], P('ax', 'rad'), may hold values from -6 to 6
- block_cols: int32 [64, 512, 4], P('ax', 'rad'), may hold values from 0 to 511
- block_kinds: int32 [64, 512, 4], P('ax', 'rad'), may hold values from 0 to 7
- block_table: float32 [8, 128, 128], replicated, may hold values from -0.5 to 0.5
- send_axial: int32 [64, 8, 2, 64], P('ax', 'rad'), may hold values from 0 to 2047, as said below
- send_radial: int32 [64, 8, 2, 32], P('ax', 'rad'), may hold values from 0 to 2047, as said below
- send_counts: int32 [64, 8, 4], P('ax', 'rad'), may hold values from 0 to 64, as said below
Outputs:
- motion_out: float32 [6, 1048576], P(None, ('ax', 'rad'))
- arrivals_axial: float32 [64, 8, 2, 7, 64], P('ax', 'rad')
- arrivals_radial: float32 [64, 8, 2, 7, 32], P('ax', 'rad')
- gas_out: float32 [3, 1024, 4096], P(None, 'ax', 'rad')
- liquid_load: float32 [1024, 4096], P('ax', 'rad')
- pressure_image: float32 [1024, 4096], P('ax', 'rad')
Inputs may be any that keep to these rules, and one draw needn't show every extreme that they name: `parcel_block`: most of a device's parcel blocks lie in cell blocks of its own radial group; the others lie in other radial groups of the slab. `send_axial`: each device's lists (both axial and both radial together) hold distinct indices of that device's parcels; entries past the counts are unused. `send_radial`: disjoint from the device's axial lists, see send_axial. `send_counts`: axial counts are at most 64, radial ones at most 32; devices of radial group 0 send full lists in all four directions.
All inputs are finite; a program needn't handle non-finite values.
Results may differ from a plain program's by a relative error of at most 0.000084.
Values sent between devices are 32-bit elements; how exact they have to be, the bound alone decides.
A program may use at most 64 MiB of HBM per device.

v0:
```python
import jax
import jax.numpy as jnp
from jax import lax
from jax.sharding import PartitionSpec as P

BLOCK = 128
PARCEL_GROUP = 64
NT = 8


TOP_PRECISION = lax.Precision.HIGHEST
DRAG = 0.5
STEP = 0.5
DIAG = 6.0


def from_behind(value, axis, steps):
    count = lax.axis_size(axis)
    leading, last = (max(0, -steps), min(count, count - steps))
    return lax.ppermute(value, axis, [(source, source + steps) for source in range(leading, last)])


def with_halo(x, sides, width):
    for axis, dim in sides:
        count, length = (lax.axis_size(axis), x.shape[dim])
        up = [(i, (i + 1) % count) for i in range(count - 1)]
        down = [(j, i) for i, j in up]
        last = lax.slice_in_dim(x, length - width, length, axis=dim)
        leading = lax.slice_in_dim(x, 0, width, axis=dim)
        before = lax.ppermute(last, axis, up)
        after = lax.ppermute(leading, axis, down)
        x = jnp.concatenate([before, x, after], axis=dim)
    return x


def pass_axial(payload, offset):
    return from_behind(payload, "ax", offset)


def pass_radial(payload, offset):
    return from_behind(payload, "rad", offset)


def on_device(
    parcel_motion,
    parcel_size,
    parcel_block,
    parcel_offset,
    gas_velocity,
    pressure,
    block_cols,
    block_kinds,
    block_table,
    send_axial,
    send_radial,
    send_counts,
):
    blocks_here = pressure.shape[0] * pressure.shape[1] // BLOCK
    gas_local = gas_velocity.reshape(3, blocks_here, BLOCK)
    pres_local = pressure.reshape(blocks_here, BLOCK)
    parcel_groups = parcel_block.shape[0]
    gas_slab, pres_slab = (
        lax.all_gather(gas_local, "rad", axis=1, tiled=True),
        lax.all_gather(pres_local, "rad", axis=0, tiled=True),
    )
    gas_lookup = gas_slab[:, parcel_block, :]
    offsets = parcel_offset.reshape(parcel_groups, PARCEL_GROUP)
    block_selector = (offsets[:, :, None] == jnp.arange(BLOCK, dtype=jnp.int32)).astype(jnp.float32)
    visited_flags = jnp.einsum(
        "fpm,pkm->fpk", gas_lookup, block_selector, precision=TOP_PRECISION
    ).reshape(3, parcel_groups * PARCEL_GROUP)
    velocity = parcel_motion[3:6]
    factor = jnp.exp(-DRAG / (parcel_size * parcel_size))
    new_vel = visited_flags + (velocity - visited_flags) * factor
    new_pos = parcel_motion[0:3] + STEP * new_vel
    motion_out = jnp.concatenate([new_pos, new_vel], axis=0)
    mass = parcel_size * parcel_size * parcel_size
    deposit = jnp.concatenate([-mass * (new_vel - velocity), mass[None]], axis=0)
    deposit = deposit.reshape(4, parcel_groups, PARCEL_GROUP)
    dep_flat = jnp.einsum("cbj,bjn->bcn", deposit, block_selector, precision=TOP_PRECISION).reshape(
        parcel_groups, 4 * BLOCK
    )
    rows_here = jnp.arange(blocks_here * lax.axis_size("rad"), dtype=jnp.int32)
    hits = (parcel_block[None, :] == rows_here[:, None]).astype(jnp.float32)
    summed = lax.psum_scatter(
        jnp.dot(hits, dep_flat, precision=TOP_PRECISION), "rad", scatter_dimension=0, tiled=True
    )
    sources = summed.reshape(blocks_here, 4, BLOCK).transpose(1, 0, 2)
    gas_out = gas_velocity + sources[:3].reshape(gas_velocity.shape)
    liquid_load = sources[3].reshape(pressure.shape)
    state = jnp.concatenate([motion_out, parcel_size[None]], axis=0)
    counts = send_counts[0, 0]

    def pack(lists, live_counts):
        taken = jnp.moveaxis(jnp.take(state, lists, axis=1), 1, 0)
        live = jnp.arange(lists.shape[1], dtype=jnp.int32)[None, :] < live_counts[:, None]
        return jnp.where(live[:, None, :], taken, jnp.float32(0.0))

    out_ax = pack(send_axial[0, 0], counts[0:2])
    arrivals_axial = jnp.stack([pass_axial(out_ax[0], 1), pass_axial(out_ax[1], -1)], axis=0)[
        None, None
    ]
    out_rad = pack(send_radial[0, 0], counts[2:4])
    arrivals_radial = jnp.stack([pass_radial(out_rad[0], 1), pass_radial(out_rad[1], -1)], axis=0)[
        None, None
    ]
    padded = with_halo(pressure, (("ax", 0),), 1)
    image = DIAG * pressure - padded[2:] - padded[:-2]
    picked = pres_slab[block_cols[0]]
    kinds = (block_kinds[0][..., None] == jnp.arange(NT, dtype=jnp.int32)).astype(jnp.float32)
    grouped = jnp.einsum("bkt,bkn->btn", kinds, picked, precision=TOP_PRECISION)
    coupled = jnp.einsum("btn,tmn->bm", grouped, block_table, precision=TOP_PRECISION)
    pressure_image = image + coupled.reshape(pressure.shape)
    return (motion_out, arrivals_axial, arrivals_radial, gas_out, liquid_load, pressure_image)


def solution(mesh):
    return jax.shard_map(
        on_device,
        mesh=mesh,
        in_specs=(
            P(None, ("ax", "rad")),
            P(("ax", "rad")),
            P(("ax", "rad")),
            P(("ax", "rad")),
            P(None, "ax", "rad"),
            P("ax", "rad"),
            P("ax", "rad", None),
            P("ax", "rad", None),
            P(),
            P("ax", "rad", None, None),
            P("ax", "rad", None, None),
            P("ax", "rad", None),
        ),
        out_specs=(
            P(None, ("ax", "rad")),
            P("ax", "rad", None, None, None),
            P("ax", "rad", None, None, None),
            P(None, "ax", "rad"),
            P("ax", "rad"),
            P("ax", "rad"),
        ),
        check_vma=False,
    )
```

profile of v0, /device:TPU:280, one launch (start us, length us, event | category | flops | bytes accessed | tf_op | source)
XLA Modules:
  0.0 99.0 jit_solution(3269439988784230751)
XLA Ops:
  7.2 0.8 multiply_multiply_fusion
  8.1 0.9 reshape.182
  9.0 15.7 %all_gather.6 = f32[3,512,128]{2,1,0:T(8,128)S(1)} all-gather(f32[3,64,128]{2,1,0:T(8,128)S(1)} %reshape.182), channel_id=1, replica_groups=mesh['ax'=64,'rad'=8] {'rad'}, dimensions={1}, use_global_device_ids=true | all-gather | bytes 884736 | tf_op jit(solution)/shard_map/all_gather | solution.py:63
  25.9 1.0 convolution_bitcast_fusion
  27.0 0.7 copy-done.3
  27.8 0.7 copy-done.4
  30.7 2.2 %collective-permute-start.2 = (f32[7,32]{1,0:T(8,128)S(1)}, f32[7,32]{1,0:T(8,128)S(1)}, u32[]{:S(2)}, u32[]{:S(2)}) collective-permute-start(f32[7,32]{1,0:T(8,128)S(1)} %get-tuple-element.31), channel_id=1, source_target_pairs={{0,1},{1,2},{2,3},{3,4},{4,5},{5,6},{6,7},{8,9},{9,10},{10,11},{11... | collective-permute-start | bytes 2696 | tf_op jit(solution)/shard_map/ppermute | solution.py:20
  33.0 3.3 %collective-permute-start.3 = (f32[7,32]{1,0:T(8,128)S(1)}, f32[7,32]{1,0:T(8,128)S(1)}, u32[]{:S(2)}, u32[]{:S(2)}) collective-permute-start(f32[7,32]{1,0:T(8,128)S(1)} %get-tuple-element.32), channel_id=1, source_target_pairs={{1,0},{2,1},{3,2},{4,3},{5,4},{6,5},{7,6},{9,8},{10,9},{11,10},{12... | collective-permute-start | bytes 2696 | tf_op jit(solution)/shard_map/ppermute | solution.py:20
  36.5 0.7 fusion
  37.2 1.6 %fusion.4 = f32[512,512]{1,0:T(8,128)} fusion(s32[32]{0:T(128)S(1)} %copy-done.11, f32[4,8,4,128]{3,2,1,0:T(4,128)S(1)} %bitcast.62), kind=kOutput, calls=%fused_computation.12 | convolution fusion | flops 100679680 | bytes 1114240 | tf_op jit(solution)/shard_map/dot_general | solution.py:86
  38.8 0.7 copy-done.7
  39.6 0.6 gather_fusion.1
  40.4 3.4 %collective-permute-start = (f32[7,64]{1,0:T(8,128)S(1)}, f32[7,64]{1,0:T(8,128)S(1)}, u32[]{:S(2)}, u32[]{:S(2)}) collective-permute-start(f32[7,64]{1,0:T(8,128)S(1)} %get-tuple-element.33), channel_id=1, source_target_pairs={{0,8},{8,16},{16,24},{24,32},{32,40},{40,48},{48,56},{56,64},{64,7... | collective-permute-start | bytes 5384 | tf_op jit(solution)/shard_map/ppermute | solution.py:20
  43.8 10.6 %collective-permute-start.1 = (f32[7,64]{1,0:T(8,128)S(1)}, f32[7,64]{1,0:T(8,128)S(1)}, u32[]{:S(2)}, u32[]{:S(2)}) collective-permute-start(f32[7,64]{1,0:T(8,128)S(1)} %get-tuple-element.34), channel_id=1, source_target_pairs={{8,0},{16,8},{24,16},{32,24},{40,32},{48,40},{56,48},{64,56},{72,6... | collective-permute-start | bytes 5384 | tf_op jit(solution)/shard_map/ppermute | solution.py:20
  54.4 1.9 %collective-permute-start.4 = (f32[1,512]{1,0:T(1,128)S(1)}, f32[1,512]{1,0:T(1,128)S(1)}, u32[]{:S(2)}, u32[]{:S(2)}) collective-permute-start(f32[1,512]{1,0:T(1,128)S(1)} %get-tuple-element.26), channel_id=1, source_target_pairs={{8,0},{16,8},{24,16},{32,24},{40,32},{48,40},{56,48},{64,56},{72,6... | collective-permute-start | bytes 6152 | tf_op jit(solution)/shard_map/ppermute | solution.py:31
  57.1 14.8 %all_gather.7 = f32[512,128]{1,0:T(8,128)S(1)} all-gather(f32[64,128]{1,0:T(8,128)S(1)} %reshape.187), channel_id=1, replica_groups=mesh['ax'=64,'rad'=8] {'rad'}, dimensions={0}, use_global_device_ids=true | all-gather | bytes 294912 | tf_op jit(solution)/shard_map/all_gather | solution.py:64
  71.9 0.7 gather_fusion.3
  72.7 0.6 pad_maximum_fusion
  73.9 0.7 convolution_bitcast_fusion.1
  74.6 3.5 %collective-permute-start.5 = (f32[1,512]{1,0:T(1,128)S(1)}, f32[1,512]{1,0:T(1,128)S(1)}, u32[]{:S(2)}, u32[]{:S(2)}) collective-permute-start(f32[1,512]{1,0:T(1,128)S(1)} %get-tuple-element.27), channel_id=1, source_target_pairs={{0,8},{8,16},{16,24},{24,32},{32,40},{40,48},{48,56},{56,64},{64,7... | collective-permute-start | bytes 6152 | tf_op jit(solution)/shard_map/ppermute | solution.py:30
  79.4 8.9 %collective-permute-done.5 = f32[1,512]{1,0:T(1,128)S(1)} collective-permute-done((f32[1,512]{1,0:T(1,128)S(1)}, f32[1,512]{1,0:T(1,128)S(1)}, u32[]{:S(2)}, u32[]{:S(2)}) %collective-permute-start.5) | collective-permute-done | bytes 2080 | tf_op jit(solution)/shard_map/ppermute | solution.py:30
  88.9 0.9 reshape.185
  90.0 0.9 copy-done.1
  90.8 0.7 add.87
  (78 shorter events, 8.2 us)
Async XLA Ops:
  7.2 66.8 %copy-start = (f32[8,128,128]{2,1,0:T(8,128)S(1)}, f32[8,128,128]{2,1,0:T(8,128)}, u32[]{:S(2)}) copy-start(f32[8,128,128]{2,1,0:T(8,128)} %param.20) | copy-start | bytes 1572868
  7.2 0.8 copy-start.5
  7.2 81.7 %reduce-scatter.2.cloned.1.call-start = ((), (), s32[]{:S(2)}) async-start(), calls=%async_computation.1 | async-start | bytes 1179648 | tf_op jit(solution)/shard_map/reduce_scatter | solution.py:85
  24.7 0.7 copy-start.11
  26.9 0.9 copy-start.3
  27.8 0.7 copy-start.4
  28.5 0.7 copy-start.6
  29.9 0.7 copy-start.10
  30.7 43.9 %collective-permute-start.2 = (f32[7,32]{1,0:T(8,128)S(1)}, f32[7,32]{1,0:T(8,128)S(1)}, u32[]{:S(2)}, u32[]{:S(2)}) collective-permute-start(f32[7,32]{1,0:T(8,128)S(1)} %get-tuple-element.31), channel_id=1, source_target_pairs={{0,1},{1,2},{2,3},{3,4},{4,5},{5,6},{6,7},{8,9},{9,10},{10,11},{11... | collective-permute-start | bytes 2696 | tf_op jit(solution)/shard_map/ppermute | solution.py:20
  33.0 45.1 %collective-permute-start.3 = (f32[7,32]{1,0:T(8,128)S(1)}, f32[7,32]{1,0:T(8,128)S(1)}, u32[]{:S(2)}, u32[]{:S(2)}) collective-permute-start(f32[7,32]{1,0:T(8,128)S(1)} %get-tuple-element.32), channel_id=1, source_target_pairs={{1,0},{2,1},{3,2},{4,3},{5,4},{6,5},{7,6},{9,8},{10,9},{11,10},{12... | collective-permute-start | bytes 2696 | tf_op jit(solution)/shard_map/ppermute | solution.py:20
  38.8 0.7 copy-start.7
  40.3 14.1 %copy-start.2 = (f32[16,512]{1,0:T(8,128)S(1)}, f32[16,512]{1,0:T(8,128)}, u32[]{:S(2)}) copy-start(f32[16,512]{1,0:T(8,128)} %param.17) | copy-start | bytes 98308
  40.4 38.3 %collective-permute-start = (f32[7,64]{1,0:T(8,128)S(1)}, f32[7,64]{1,0:T(8,128)S(1)}, u32[]{:S(2)}, u32[]{:S(2)}) collective-permute-start(f32[7,64]{1,0:T(8,128)S(1)} %get-tuple-element.33), channel_id=1, source_target_pairs={{0,8},{8,16},{16,24},{24,32},{32,40},{40,48},{48,56},{56,64},{64,7... | collective-permute-start | bytes 5384 | tf_op jit(solution)/shard_map/ppermute | solution.py:20
  43.8 34.9 %collective-permute-start.1 = (f32[7,64]{1,0:T(8,128)S(1)}, f32[7,64]{1,0:T(8,128)S(1)}, u32[]{:S(2)}, u32[]{:S(2)}) collective-permute-start(f32[7,64]{1,0:T(8,128)S(1)} %get-tuple-element.34), channel_id=1, source_target_pairs={{8,0},{16,8},{24,16},{32,24},{40,32},{48,40},{56,48},{64,56},{72,6... | collective-permute-start | bytes 5384 | tf_op jit(solution)/shard_map/ppermute | solution.py:20
  54.4 2.0 %copy-start.9 = (s32[1,64,4]{1,2,0:T(4,128)S(1)}, s32[1,64,4]{1,2,0:T(4,128)}, u32[]{:S(2)}) copy-start(s32[1,64,4]{1,2,0:T(4,128)} %param.18) | copy-start | bytes 3076
  54.4 25.0 %collective-permute-start.4 = (f32[1,512]{1,0:T(1,128)S(1)}, f32[1,512]{1,0:T(1,128)S(1)}, u32[]{:S(2)}, u32[]{:S(2)}) collective-permute-start(f32[1,512]{1,0:T(1,128)S(1)} %get-tuple-element.26), channel_id=1, source_target_pairs={{8,0},{16,8},{24,16},{32,24},{40,32},{48,40},{56,48},{64,56},{72,6... | collective-permute-start | bytes 6152 | tf_op jit(solution)/shard_map/ppermute | solution.py:31
  56.4 0.7 copy-start.8
  74.6 13.6 %collective-permute-start.5 = (f32[1,512]{1,0:T(1,128)S(1)}, f32[1,512]{1,0:T(1,128)S(1)}, u32[]{:S(2)}, u32[]{:S(2)}) collective-permute-start(f32[1,512]{1,0:T(1,128)S(1)} %get-tuple-element.27), channel_id=1, source_target_pairs={{0,8},{8,16},{16,24},{24,32},{32,40},{40,48},{48,56},{56,64},{64,7... | collective-permute-start | bytes 6152 | tf_op jit(solution)/shard_map/ppermute | solution.py:30
  89.9 0.9 copy-start.1
Sparse Core Ops, SparseCore 0:
  39.0 37.3 reduce-scatter.1
where the time goes:
time: 99.7 us; the launch traced here: 99 us
  blocking collectives  30.5 us (31%)
  starting transfers between devices  24.9 us (25%)
  between operations  14.4 us (14%)
  local copies, waits for them, and re-layouts  11.6 us (12%)
  waiting for transfers between devices  8.9 us (9%)
  matrix products  4.55 us (5%)
  other arithmetic  4.18 us (4%)
    ppermute x4, starting transfers between devices, from_behind(): lax.ppermute(value, axis, [(source, source + steps) for source in range(l...  19.5 us
    all_gather x1, blocking collectives, on_device(): lax.all_gather(gas_local, 'rad', axis=1, tiled=True)  15.7 us
    all_gather x1, blocking collectives, on_device(): lax.all_gather(pres_local, 'rad', axis=0, tiled=True)  14.8 us
    ppermute x1, waiting for transfers between devices, with_halo(): before = lax.ppermute(last, axis, up)  8.86 us
    unnamed x24, local copies, waits for them, and re-layouts  4.38 us
    ppermute x1, starting transfers between devices, with_halo(): before = lax.ppermute(last, axis, up)  3.45 us
  transfers between devices with their start and end apart: 7, of which 1 were waited for; matrix products, arithmetic and copies ran while one was open for 8% of the time, Pallas kernels for 0%

commit v1 on v0

v1 whole, which is shorter than its diff:
```python
import functools

import jax
import jax.numpy as jnp
from jax import lax
from jax.experimental import pallas as pl
from jax.experimental.pallas import tpu as pltpu
from jax.sharding import PartitionSpec as P

MESH = pl.DeviceIdType.MESH
F32 = jnp.float32
BF16 = jnp.bfloat16
I32 = jnp.int32
HIGHEST = lax.Precision.HIGHEST
SLOTS = 16
VMEM_BYTES = 62 * 1024 * 1024
NT_DIMS = (((1,), (1,)), ((), ()))


def hdot(a, b):
    return jnp.dot(a, b, precision=HIGHEST, preferred_element_type=F32)


def split3(x):
    hi = x.astype(BF16)
    rest = x - hi.astype(F32)
    mid = rest.astype(BF16)
    lo = (rest - mid.astype(F32)).astype(BF16)
    return hi, mid, lo


def iota(shape, dim):
    return lax.broadcasted_iota(I32, shape, dim)


def lane_gather(x, index):
    return jnp.take_along_axis(x, index, axis=1)


def step_kernel(
    na,
    nr,
    pm,
    ps,
    pb,
    po,
    gas,
    pres,
    cols,
    kinds,
    table,
    sa,
    sr,
    sc,
    motion_o,
    arra_o,
    arrr_o,
    gas_o,
    liq_o,
    pim_o,
    pmv,
    psv,
    pbv,
    pov,
    gasv,
    colv,
    kindv,
    tabv,
    sav,
    srv,
    scv,
    slab,
    rows8,
    rq,
    rqs,
    rp,
    rps,
    state,
    uown,
    dp,
    sd,
    sds,
    halo,
    xs,
    xa,
    xr,
    keys,
    coup,
    p3,
    motv,
    arrav,
    arrrv,
    gasov,
    liqv,
    pimv,
    lsem,
    osem,
    rq_s,
    rq_r,
    rp_s,
    rp_r,
    pr_s,
    pr_r,
    sd_s,
    sd_r,
    ha_s,
    ha_r,
    x_s,
    x_r,
):
    a = lax.axis_index("ax")
    r = lax.axis_index("rad")
    has_prev, has_next = a > 0, a < na - 1
    has_in, has_out = r > 0, r < nr - 1

    def to(src, dst, ssem, rsem, **where):
        return pltpu.make_async_remote_copy(
            src_ref=src, dst_ref=dst, send_sem=ssem, recv_sem=rsem, device_id=where, device_id_type=MESH
        )

    barrier = pltpu.get_barrier_semaphore()
    for k in range(1, nr):
        pl.semaphore_signal(barrier, inc=1, device_id={"rad": lax.rem(r + k, nr)}, device_id_type=MESH)

    @pl.when(has_prev)
    def _():
        pl.semaphore_signal(barrier, inc=1, device_id={"ax": a - 1}, device_id_type=MESH)

    @pl.when(has_next)
    def _():
        pl.semaphore_signal(barrier, inc=1, device_id={"ax": a + 1}, device_id_type=MESH)

    loads = [
        pltpu.make_async_copy(src, dst, lsem.at[i])
        for i, (src, dst) in enumerate(
            (
                (pb, pbv),
                (po, pov),
                (gas, gasv),
                (ps, psv),
                (pm, pmv),
                (sa, sav),
                (sr, srv),
                (sc, scv),
                (pres, slab.at[r]),
                (cols, colv),
                (kinds, kindv),
                (table, tabv),
            )
        )
    ]
    for load in loads:
        load.start()

    lane8 = iota((8, 128), 1)
    sub8 = iota((8, 128), 0)
    lane16 = iota((16, 128), 1)
    low8 = lane8 < 64
    low16 = lane16 < 64

    rows8[...] = jnp.zeros((8, 128), I32)
    loads[0].wait()
    loads[1].wait()
    rows8[0:1, 0:32] = pbv[...]
    blocks = jnp.broadcast_to(rows8[0:1, :], (8, 128))
    order = jnp.bitwise_and(jnp.where(lane8 < 16, 2 * lane8, 2 * lane8 - 31), 127)
    blocks = lane_gather(blocks, order)
    owner = jnp.right_shift(blocks, 6)
    local = jnp.bitwise_and(blocks, 63)
    ident = owner * 64 + jnp.bitwise_and(local, 3) * 16 + jnp.right_shift(local, 2)
    valid = lane8 < 32
    away = jnp.where(valid & (owner != r), 1, 0)
    rank = away
    for s in (1, 2, 4, 8, 16):
        rank = rank + jnp.where(lane8 >= s, pltpu.roll(rank, s, axis=1), 0)
    rank = rank - away
    row_rank = jnp.where(away > 0, rank, -1)
    code = jnp.where(valid, (rank * 2 + away) * 1024 + ident, 0)
    col = jnp.transpose(jnp.broadcast_to(code[0:1, :], (128, 128)))[0:32, :]
    col_id = jnp.bitwise_and(col, 1023)
    col_away = jnp.bitwise_and(jnp.right_shift(col, 10), 1)
    col_rank = jnp.right_shift(col, 11)
    lane32 = iota((32, 128), 1)
    picked = jnp.where((col_away > 0) & (col_rank + SLOTS * r == lane32), col_id + 1, 0)
    ids = picked[0:8] + picked[8:16] + picked[16:24] + picked[24:32]
    for s in (4, 2, 1):
        ids = ids + pltpu.roll(ids, s, axis=0)
    to_slot = jnp.where(
        jnp.broadcast_to(row_rank[0:1, :], (SLOTS, 128)) == iota((SLOTS, 128), 0), 1.0, 0.0
    ).astype(F32)[:, 0:32]
    offsets = pov[...]
    offs_f = offsets.astype(F32)
    slot_offs = jnp.dot(
        to_slot.astype(BF16),
        jnp.concatenate([offs_f, pltpu.roll(offs_f, 64, axis=1)], axis=0).astype(BF16),
        preferred_element_type=F32,
    ).astype(I32)
    rqs[0:8, :] = jnp.where(low8, slot_offs[0:8], pltpu.roll(slot_offs[8:16], 64, axis=1))
    rqs[8:16, :] = ids

    rq[r] = jnp.zeros((16, 128), I32)
    rp[r] = jnp.zeros((3, 8, 128), F32)
    sd[r] = jnp.zeros((4, SLOTS, 128), F32)

    @pl.when(jnp.logical_not(has_prev))
    def _():
        xa[0] = jnp.zeros((8, 128), F32)
        halo[0] = jnp.zeros((8, 512), F32)

    @pl.when(jnp.logical_not(has_next))
    def _():
        xa[1] = jnp.zeros((8, 128), F32)
        halo[1] = jnp.zeros((8, 512), F32)

    @pl.when(jnp.logical_not(has_in))
    def _():
        xr[0] = jnp.zeros((8, 128), F32)

    @pl.when(jnp.logical_not(has_out))
    def _():
        xr[1] = jnp.zeros((8, 128), F32)

    pl.semaphore_wait(barrier, nr - 1 + has_prev.astype(I32) + has_next.astype(I32))

    requests = []
    for k in range(1, nr):
        c = to(rqs, rq.at[r], rq_s.at[k], rq_r.at[k], rad=lax.rem(r + k, nr))
        c.start()
        requests.append(c)

    def halo_next():
        return to(pres.at[8:16], halo.at[0], ha_s.at[0], ha_r.at[0], ax=a + 1)

    def halo_prev():
        return to(pres.at[0:8], halo.at[1], ha_s.at[1], ha_r.at[1], ax=a - 1)

    @pl.when(has_next)
    def _():
        halo_next().start()

    @pl.when(has_prev)
    def _():
        halo_prev().start()

    loads[2].wait()
    gas_rows = jnp.concatenate(
        [
            jnp.concatenate([gasv[c, :, 128 * q : 128 * q + 128] for q in range(4)], axis=0)
            for c in range(3)
        ],
        axis=1,
    )
    at_own = jnp.where(col_id == r * 64 + lane32, 1.0, 0.0).astype(F32)[:, 0:64]
    found = hdot(at_own, gas_rows)
    for c in range(3):
        part = found[:, 128 * c : 128 * c + 128]
        uown[c] = jnp.where(low16, lane_gather(part[0:16], offsets), lane_gather(part[16:32], offsets))

    for c in requests:
        c.wait_recv()
    asked = rq[0, 8:16, :]
    for s in range(1, nr):
        asked = asked + rq[s, 8:16, :]
    asked_col = jnp.transpose(jnp.broadcast_to(asked[0:1, :], (128, 128)))
    at_asked = jnp.where(asked_col == r * 64 + 1 + iota((128, 128), 1), 1.0, 0.0).astype(F32)[:, 0:64]
    found = hdot(at_asked, gas_rows)
    for s in range(nr):
        index = rq[s, 0:8, :]
        for c in range(3):
            part = found[SLOTS * s : SLOTS * s + 16, 128 * c : 128 * c + 128]
            rps[s, c] = jnp.where(low8, lane_gather(part[0:8], index), lane_gather(part[8:16], index))
    replies = []
    for k in range(1, nr):
        dst = lax.rem(r + k, nr)
        c = to(rps.at[dst], rp.at[r], rp_s.at[k], rp_r.at[k], rad=dst)
        c.start()
        replies.append(c)
    shares = []
    for k in range(1, nr):
        c = to(pres, slab.at[r], pr_s.at[k], pr_r.at[k], rad=lax.rem(r + k, nr))
        c.start()
        shares.append(c)

    loads[9].wait()
    loads[10].wait()
    cv = colv[0]
    key = kindv[0] * 512 + jnp.bitwise_and(cv, 3) * 128 + jnp.right_shift(cv, 6) * 16
    key = key + jnp.bitwise_and(jnp.right_shift(cv, 2), 15)
    rows8[4:8, 0:64] = key
    for k in range(4):
        keys[k] = jnp.transpose(jnp.broadcast_to(rows8[4 + k : 5 + k, :], (128, 128)))[0:64, :]

    loads[3].wait()
    size = psv[...]
    factor = jnp.exp(-0.5 / (size * size))
    mass = size * size * size
    loads[4].wait()
    for i in (5, 6, 7):
        loads[i].wait()
    rows8[0:2, 0:64] = sav[0, 0]
    rows8[2:4, 0:32] = srv[0, 0]
    lists = [jnp.broadcast_to(rows8[i : i + 1, :], (8, 128)) for i in range(4)]
    counts = [jnp.broadcast_to(scv[0, :, i : i + 1], (8, 128)) for i in range(4)]
    list_ax = jnp.where(low8, lists[0], pltpu.roll(lists[1], 64, axis=1))
    list_rad = jnp.where(low8, lists[2], pltpu.roll(lists[3], 64, axis=1))
    live_ax = lane8 < jnp.where(low8, counts[0], counts[1] + 64)
    live_rad = lane8 < jnp.where(low8, counts[2], counts[3] + 64)

    w_lo = jnp.where((col_away > 0) & (col_rank < 8) & (jnp.right_shift(col_id, 6) * 8 + col_rank == lane32), 1.0, 0.0)
    w_hi = jnp.where((col_away > 0) & (col_rank >= 8) & (jnp.right_shift(col_id, 6) * 8 + col_rank - 8 == lane32), 1.0, 0.0)
    w = jnp.concatenate([w_lo, w_hi], axis=0).astype(F32)[:, 0:64]

    for c in replies:
        c.wait_recv()
    answer = jnp.concatenate([rp[:, c].reshape(nr * 8, 128) for c in range(3)], axis=1)
    spread = hdot(w, answer)
    u = []
    for c in range(3):
        lo, hi = spread[0:32, 128 * c : 128 * c + 128], spread[32:64, 128 * c : 128 * c + 128]
        even = lo[0:16] + pltpu.roll(hi[0:16], 64, axis=1)
        odd = pltpu.roll(lo[16:32], 64, axis=1) + hi[16:32]
        u.append(uown[c] + jnp.where(low16, even, odd))

    cross_ax = jnp.zeros((8, 128), F32)
    cross_rad = jnp.zeros((8, 128), F32)
    tile_ax, lane_ax = jnp.right_shift(list_ax, 7), jnp.bitwise_and(list_ax, 127)
    tile_rad, lane_rad = jnp.right_shift(list_rad, 7), jnp.bitwise_and(list_rad, 127)
    is_vel = (sub8 >= 3) & (sub8 < 6)
    for t in range(16):
        row = lambda x: jnp.broadcast_to(x[t : t + 1, :], (8, 128))
        old = jnp.concatenate([pmv[:, 128 * t : 128 * t + 128], jnp.zeros((2, 128), F32)], axis=0)
        gas_t = jnp.where(sub8 == 3, row(u[0]), jnp.where(sub8 == 4, row(u[1]), row(u[2])))
        vel = gas_t + (old - gas_t) * row(factor)
        pos = old + 0.5 * pltpu.roll(vel, 5, axis=0)
        new = jnp.where(sub8 < 3, pos, jnp.where(is_vel, vel, row(size)))
        motv[:, 128 * t : 128 * t + 128] = new[0:6]
        m = row(mass)
        state[:, 128 * t : 128 * t + 128] = jnp.where(is_vel, -m * (vel - old), jnp.where(sub8 == 6, m, 0.0))
        cross_ax = jnp.where(tile_ax == t, lane_gather(new, lane_ax), cross_ax)
        cross_rad = jnp.where(tile_rad == t, lane_gather(new, lane_rad), cross_rad)
    cross_ax = jnp.where(live_ax, cross_ax, 0.0)
    cross_rad = jnp.where(live_rad, cross_rad, 0.0)
    xs[0] = cross_ax
    xs[1] = pltpu.roll(cross_ax, 64, axis=1)
    xs[2] = cross_rad
    xs[3] = pltpu.roll(cross_rad, 64, axis=1)

    def crossing(i):
        dst = (xa.at[0], xa.at[1], xr.at[0], xr.at[1])[i]
        where = ({"ax": a + 1}, {"ax": a - 1}, {"rad": r + 1}, {"rad": r - 1})[i]
        return to(xs.at[i], dst, x_s.at[i], x_r.at[i], **where)

    sends_to = (has_next, has_prev, has_out, has_in)
    comes_from = (has_prev, has_next, has_in, has_out)
    for i in range(4):

        @pl.when(sends_to[i])
        def _(i=i):
            crossing(i).start()

    out_motion = pltpu.make_async_copy(motv, motion_o, osem.at[0])
    out_motion.start()

    sub128 = iota((128, 128), 0)
    for t in range(16):
        d = state[:, 128 * t : 128 * t + 128]
        both = jnp.concatenate([jnp.where(low8, d, 0.0), jnp.where(low8, 0.0, d)], axis=0)
        cells = jnp.where(
            jnp.broadcast_to(offsets[t : t + 1, :], (128, 128)) == sub128, 1.0, 0.0
        ).astype(BF16)
        sums = lax.dot_general(
            jnp.concatenate(split3(both), axis=0), cells, NT_DIMS, preferred_element_type=F32
        )
        sums = sums[0:16] + sums[16:32] + sums[32:48]
        dp[t] = sums[0:8]
        dp[16 + t] = sums[8:16]
    by_comp = jnp.concatenate([dp[:, 3 + c, :] for c in range(4)], axis=1)
    slotted = hdot(to_slot, by_comp)
    for c in range(4):
        sds[c] = slotted[:, 128 * c : 128 * c + 128]
    deposits = []
    for k in range(1, nr):
        c = to(sds, sd.at[r], sd_s.at[k], sd_r.at[k], rad=lax.rem(r + k, nr))
        c.start()
        deposits.append(c)

    loads[8].wait()
    loads[11].wait()
    for c in shares:
        c.wait_recv()
    slab_rows = jnp.concatenate(
        [slab[:, :, 128 * q : 128 * q + 128].reshape(nr * 16, 128) for q in range(4)], axis=0
    )
    p3[...] = jnp.concatenate(split3(slab_rows), axis=1)
    coup[...] = jnp.zeros((64, 128), F32)
    lane64 = iota((64, 128), 1)

    def kind_step(t, carry):
        chosen = []
        for q in range(4):
            want = t * 512 + q * 128 + lane64
            g = jnp.where(keys[0] == want, 1.0, 0.0)
            for k in range(1, 4):
                g = g + jnp.where(keys[k] == want, 1.0, 0.0)
            chosen.append(g.astype(BF16))
        three = jnp.dot(jnp.concatenate(chosen, axis=1), p3[...], preferred_element_type=F32)
        grouped = three[:, 0:128] + three[:, 128:256] + three[:, 256:384]
        coup[...] += lax.dot_general(
            grouped, tabv[t], NT_DIMS, precision=HIGHEST, preferred_element_type=F32
        )
        return carry

    lax.fori_loop(0, 8, kind_step, 0)

    for c in deposits:
        c.wait_recv()
    row_id = jnp.broadcast_to(jnp.where(valid, ident, -1)[0:1, :], (64, 128))
    sub64 = iota((64, 128), 0)
    hits_own = jnp.where(row_id == r * 64 + sub64, 1.0, 0.0).astype(F32)[:, 0:32]
    hits_far = jnp.where(jnp.broadcast_to(asked[0:1, :], (64, 128)) == r * 64 + 1 + sub64, 1.0, 0.0).astype(F32)
    far = jnp.concatenate([sd[:, c].reshape(nr * SLOTS, 128) for c in range(4)], axis=1)
    sources = hdot(hits_own, by_comp) + hdot(hits_far, far)
    for q in range(4):
        rows = slice(16 * q, 16 * q + 16)
        lanes = slice(128 * q, 128 * q + 128)
        for c in range(3):
            gasov[c, :, lanes] = gasv[c, :, lanes] + sources[rows, 128 * c : 128 * c + 128]
        liqv[:, lanes] = sources[rows, 384:512]
    outs = [pltpu.make_async_copy(gasov, gas_o, osem.at[1]), pltpu.make_async_copy(liqv, liq_o, osem.at[2])]
    for c in outs:
        c.start()

    @pl.when(has_prev)
    def _():
        to(pres.at[8:16], halo.at[0], ha_s.at[0], ha_r.at[0], ax=a - 1).wait_recv()

    @pl.when(has_next)
    def _():
        to(pres.at[0:8], halo.at[1], ha_s.at[1], ha_r.at[1], ax=a + 1).wait_recv()

    mine = slab[r]
    above = jnp.concatenate([halo[0, 7:8, :], mine[0:15]], axis=0)
    below = jnp.concatenate([mine[1:16], halo[1, 0:1, :]], axis=0)
    image = 6.0 * mine - below - above
    for q in range(4):
        lanes = slice(128 * q, 128 * q + 128)
        pimv[:, lanes] = image[:, lanes] + coup[pl.ds(q, 16, stride=4), :]
    outs.append(pltpu.make_async_copy(pimv, pim_o, osem.at[3]))
    outs[-1].start()

    for i in range(4):

        @pl.when(comes_from[i])
        def _(i=i):
            crossing(i).wait_recv()

    for i in range(2):
        for f in range(7):
            arrav[0, 0, f, i : i + 1, :] = xa[i, f : f + 1, 0:64]
            arrrv[0, 0, f, i : i + 1, :] = xr[i, f : f + 1, 0:32]
    outs.append(pltpu.make_async_copy(arrav, arra_o, osem.at[4]))
    outs.append(pltpu.make_async_copy(arrrv, arrr_o, osem.at[5]))
    outs[-2].start()
    outs[-1].start()

    for c in requests + replies + shares + deposits:
        c.wait_send()

    @pl.when(has_next)
    def _():
        halo_next().wait_send()

    @pl.when(has_prev)
    def _():
        halo_prev().wait_send()

    for i in range(4):

        @pl.when(sends_to[i])
        def _(i=i):
            crossing(i).wait_send()

    out_motion.wait()
    for c in outs:
        c.wait()


def out_kernel(*refs):
    sources, targets, sem = refs[:6], refs[6:12], refs[12]
    copies = [pltpu.make_async_copy(s, t, sem.at[i]) for i, (s, t) in enumerate(zip(sources, targets))]
    for c in copies:
        c.start()
    for c in copies:
        c.wait()


def on_device(na, nr, pm, ps, pb, po, gas, pres, cols, kinds, table, sa, sr, sc):
    outs = (
        jax.ShapeDtypeStruct((6, 2048), F32),
        jax.ShapeDtypeStruct((1, 1, 7, 2, 64), F32),
        jax.ShapeDtypeStruct((1, 1, 7, 2, 32), F32),
        jax.ShapeDtypeStruct((3, 16, 512), F32),
        jax.ShapeDtypeStruct((16, 512), F32),
        jax.ShapeDtypeStruct((16, 512), F32),
    )
    V = pltpu.VMEM
    dma = pltpu.SemaphoreType.DMA
    anyspec = pl.BlockSpec(memory_space=pltpu.HBM)
    scratch = [
        V((6, 2048), F32),
        V((16, 128), F32),
        V((1, 32), I32),
        V((16, 128), I32),
        V((3, 16, 512), F32),
        V((1, 4, 64), I32),
        V((1, 4, 64), I32),
        V((8, 128, 128), F32),
        V((1, 1, 2, 64), I32),
        V((1, 1, 2, 32), I32),
        V((1, 1, 4), I32),
        V((nr, 16, 512), F32),
        V((8, 128), I32),
        V((nr, 16, 128), I32),
        V((16, 128), I32),
        V((nr, 3, 8, 128), F32),
        V((nr, 3, 8, 128), F32),
        V((8, 2048), F32),
        V((3, 16, 128), F32),
        V((32, 8, 128), F32),
        V((nr, 4, SLOTS, 128), F32),
        V((4, SLOTS, 128), F32),
        V((2, 8, 512), F32),
        V((4, 8, 128), F32),
        V((2, 8, 128), F32),
        V((2, 8, 128), F32),
        V((4, 64, 128), I32),
        V((64, 128), F32),
        V((512, 384), BF16),
        V((6, 2048), F32),
        V((1, 1, 7, 2, 64), F32),
        V((1, 1, 7, 2, 32), F32),
        V((3, 16, 512), F32),
        V((16, 512), F32),
        V((16, 512), F32),
        dma((12,)),
        dma((6,)),
        dma((8,)),
        dma((8,)),
        dma((8,)),
        dma((8,)),
        dma((8,)),
        dma((8,)),
        dma((8,)),
        dma((8,)),
        dma((2,)),
        dma((2,)),
        dma((4,)),
        dma((4,)),
    ]
    parts = pl.pallas_call(
        functools.partial(step_kernel, na, nr),
        out_shape=outs,
        in_specs=[anyspec] * 12,
        out_specs=[anyspec] * 6,
        scratch_shapes=scratch,
        compiler_params=pltpu.CompilerParams(
            collective_id=0, has_side_effects=True, vmem_limit_bytes=VMEM_BYTES
        ),
        name="step",
    )(
        pm,
        ps.reshape(16, 128),
        pb.reshape(1, 32),
        po.reshape(16, 128),
        gas,
        pres,
        jnp.swapaxes(cols, 1, 2),
        jnp.swapaxes(kinds, 1, 2),
        table,
        sa,
        sr,
        sc,
    )
    motion, axial, radial, gas_out, load, image = pl.pallas_call(
        out_kernel,
        out_shape=outs,
        in_specs=[anyspec] * 6,
        out_specs=[anyspec] * 6,
        scratch_shapes=[dma((6,))],
        compiler_params=pltpu.CompilerParams(vmem_limit_bytes=VMEM_BYTES),
        name="copy_out",
    )(*parts)
    return motion, jnp.swapaxes(axial, 2, 3), jnp.swapaxes(radial, 2, 3), gas_out, load, image


def solution(mesh):
    na, nr = mesh.shape["ax"], mesh.shape["rad"]
    return jax.shard_map(
        functools.partial(on_device, na, nr),
        mesh=mesh,
        in_specs=(
            P(None, ("ax", "rad")),
            P(("ax", "rad")),
            P(("ax", "rad")),
            P(("ax", "rad")),
            P(None, "ax", "rad"),
            P("ax", "rad"),
            P("ax", "rad", None),
            P("ax", "rad", None),
            P(),
            P("ax", "rad", None, None),
            P("ax", "rad", None, None),
            P("ax", "rad", None),
        ),
        out_specs=(
            P(None, ("ax", "rad")),
            P("ax", "rad", None, None, None),
            P("ax", "rad", None, None, None),
            P(None, "ax", "rad"),
            P("ax", "rad"),
            P("ax", "rad"),
        ),
        check_vma=False,
    )
```

time: 99.7 us -> 40.1 us (0.40)
  the two profiles are of different devices: /device:TPU:280 before, /device:TPU:393 now
where the time goes in v1:
time: 40.1 us; the launch traced here: 39.9 us
  Pallas kernels  39.3 us (98%)
  between operations  0.64 us (2%)
    pallas_call x1, Pallas kernels, on_device(): pl.pallas_call(functools.partial(step_kernel, na, nr), out_shape=outs, in...  30.7 us
    pallas_call x1, Pallas kernels, on_device(): pl.pallas_call(out_kernel, out_shape=outs, in_specs=[anyspec] * 6, out_sp...  8.54 us

profile of v1, /device:TPU:393, one launch (start us, length us, event | category | flops | bytes accessed | tf_op | source)
XLA Modules:
  0.0 39.9 jit_solution(2589055156660402556)
XLA Ops:
  0.6 30.7 %step.1 = (f32[6,2048]{1,0:T(8,128)}, f32[1,1,7,2,64]{4,3,2,1,0:T(2,128)}, f32[1,1,7,2,32]{4,3,2,1,0:T(2,128)}, f32[3,16,512]{2,1,0:T(8,128)}, f32[16,512]{1,0:T(8,128)}, /*index=5*/f32[16,512]{1,0:T(8,128)}) custom-call(f32[6,2048]{1,0:T(8,128)} %pm.1, f32[16,128]{1,0:T(8,128)} %bitcast.7, s32[1,32]{1,0:T(1,128)} %bitcast.11, s32[16,128]{1,0:T(8,128)} %bitcast.8, ...), custom_call_target="tpu_custom_call" | custom-call | tf_op jit(solution)/shard_map/step/pallas_call | solution.py:560
  31.4 8.5 %copy_out.1 = (f32[6,2048]{1,0:T(8,128)}, f32[1,1,7,2,64]{4,3,2,1,0:T(2,128)}, f32[1,1,7,2,32]{4,3,2,1,0:T(2,128)}, f32[3,16,512]{2,1,0:T(8,128)}, f32[16,512]{1,0:T(8,128)}, /*index=5*/f32[16,512]{1,0:T(8,128)}) custom-call(f32[6,2048]{1,0:T(8,128)} %get-tuple-element.18.refs_0_, f32[1,1,7,2,64]{4,3,2,1,0:T(2,128)} %get-tuple-element.19.refs_1_, ...), custom_call_target="tpu_custom_call" | custom-call | tf_op jit(solution)/shard_map/copy_out/pallas_call | solution.py:584

commit v2 on v1

--- a/solution.py
+++ b/solution.py
@@ -13,6 +13,7 @@
 I32 = jnp.int32
 HIGHEST = lax.Precision.HIGHEST
 SLOTS = 16
+ROWS = 5
 VMEM_BYTES = 62 * 1024 * 1024
 NT_DIMS = (((1,), (1,)), ((), ()))
 
@@ -27,6 +28,14 @@
     mid = rest.astype(BF16)
     lo = (rest - mid.astype(F32)).astype(BF16)
     return hi, mid, lo
+
+
+def pieces(x):
+    return jnp.concatenate(split3(x), axis=0)
+
+
+def pick(onehot, x3):
+    return jnp.dot(onehot.astype(BF16), x3, preferred_element_type=F32)
 
 
 def iota(shape, dim):
@@ -52,12 +61,12 @@
     sa,
     sr,
     sc,
-    motion_o,
-    arra_o,
-    arrr_o,
-    gas_o,
-    liq_o,
-    pim_o,
+    motv,
+    arrav,
+    arrrv,
+    gasov,
+    liqv,
+    pimv,
     pmv,
     psv,
     pbv,
@@ -75,7 +84,6 @@
     rqs,
     rp,
     rps,
-    state,
     uown,
     dp,
     sd,
@@ -87,14 +95,7 @@
     keys,
     coup,
     p3,
-    motv,
-    arrav,
-    arrrv,
-    gasov,
-    liqv,
-    pimv,
     lsem,
-    osem,
     rq_s,
     rq_r,
     rp_s,
@@ -169,6 +170,10 @@
     local = jnp.bitwise_and(blocks, 63)
     ident = owner * 64 + jnp.bitwise_and(local, 3) * 16 + jnp.right_shift(local, 2)
     valid = lane8 < 32
+
+    def thrice(x):
+        return jnp.where(lane8 < 32, x, jnp.where(lane8 < 64, pltpu.roll(x, 32, axis=1), pltpu.roll(x, 64, axis=1)))
+
     away = jnp.where(valid & (owner != r), 1, 0)
     rank = away
     for s in (1, 2, 4, 8, 16):
@@ -196,11 +201,11 @@
         preferred_element_type=F32,
     ).astype(I32)
     rqs[0:8, :] = jnp.where(low8, slot_offs[0:8], pltpu.roll(slot_offs[8:16], 64, axis=1))
-    rqs[8:16, :] = ids
+    rqs[8:9, :] = ids[0:1]
 
     rq[r] = jnp.zeros((16, 128), I32)
     rp[r] = jnp.zeros((3, 8, 128), F32)
-    sd[r] = jnp.zeros((4, SLOTS, 128), F32)
+    sd[r] = jnp.zeros((ROWS, SLOTS, 128), F32)
 
     @pl.when(jnp.logical_not(has_prev))
     def _():
@@ -222,11 +227,35 @@
 
     pl.semaphore_wait(barrier, nr - 1 + has_prev.astype(I32) + has_next.astype(I32))
 
+    core = lax.rem(r, 2)
+    sibling = r + 1 - 2 * core
+
+    def spread_out(src, dst, ssem, rsem):
+        copies = []
+        for j in range(4):
+            target = lax.rem(r + 2 * j, nr) if j else sibling
+            c = to(src, dst.at[r], ssem.at[j], rsem.at[j], rad=target)
+            c.start()
+            copies.append(c)
+        return copies
+
+    def pass_on(copies, dst, ssem, rsem):
+        again = []
+        for j in range(1, 4):
+            copies[j].wait_recv()
+            origin = dst.at[lax.rem(r + nr - 2 * j, nr)]
+            c = to(origin, origin, ssem.at[3 + j], rsem.at[3 + j], rad=sibling)
+            c.start()
+            again.append(c)
+        return again
+
     requests = []
     for k in range(1, nr):
-        c = to(rqs, rq.at[r], rq_s.at[k], rq_r.at[k], rad=lax.rem(r + k, nr))
+        c = to(rqs.at[0:9], rq.at[r, 0:9], rq_s.at[k], rq_r.at[k], rad=lax.rem(r + k, nr))
         c.start()
         requests.append(c)
+
+    shares = spread_out(pres, slab, pr_s, pr_r)
 
     def halo_next():
         return to(pres.at[8:16], halo.at[0], ha_s.at[0], ha_r.at[0], ax=a + 1)
@@ -250,20 +279,46 @@
         ],
         axis=1,
     )
-    at_own = jnp.where(col_id == r * 64 + lane32, 1.0, 0.0).astype(F32)[:, 0:64]
-    found = hdot(at_own, gas_rows)
+    gas3 = pieces(gas_rows)
+    at_own = jnp.where(col_id[:, 0:1] == r * 64 + jnp.bitwise_and(iota((32, 192), 1), 63), 1.0, 0.0)
+    found = pick(at_own, gas3)
     for c in range(3):
         part = found[:, 128 * c : 128 * c + 128]
         uown[c] = jnp.where(low16, lane_gather(part[0:16], offsets), lane_gather(part[16:32], offsets))
 
+    loads[3].wait()
+    size = psv[...]
+    factor = jnp.exp(-0.5 / (size * size))
+    mass = size * size * size
+    share = mass * (1.0 - factor)
+    loads[4].wait()
+    is_vel = (sub8 >= 3) & (sub8 < 6)
+    sub128 = iota((128, 128), 0)
+    for t in range(16):
+        row = lambda x: jnp.broadcast_to(x[t : t + 1, :], (8, 128))
+        old = jnp.concatenate([pmv[:, 128 * t : 128 * t + 128], jnp.zeros((2, 128), F32)], axis=0)
+        d = row(share) * jnp.where(is_vel, old, 1.0)
+        d = jnp.where(sub8 == 6, row(mass), d)
+        both = jnp.concatenate([jnp.where(low8, d, 0.0), jnp.where(low8, 0.0, d)], axis=0)
+        cells = jnp.where(jnp.broadcast_to(offsets[t : t + 1, :], (128, 128)) == sub128, 1.0, 0.0).astype(BF16)
+        sums = lax.dot_general(pieces(both), cells, NT_DIMS, preferred_element_type=F32)
+        sums = sums[0:16] + sums[16:32] + sums[32:48]
+        dp[t] = sums[0:8]
+        dp[16 + t] = sums[8:16]
+    own3 = pieces(jnp.concatenate([dp[:, 2 + c, :] for c in range(ROWS)], axis=1))
+    slot_of = jnp.broadcast_to(thrice(row_rank)[0:1, 0:96], (SLOTS, 96))
+    slotted = pick(jnp.where(slot_of == iota((SLOTS, 96), 0), 1.0, 0.0), own3)
+    for c in range(ROWS):
+        sds[c] = slotted[:, 128 * c : 128 * c + 128]
+
     for c in requests:
         c.wait_recv()
-    asked = rq[0, 8:16, :]
+    asked = rq[0, 8:9, :]
     for s in range(1, nr):
-        asked = asked + rq[s, 8:16, :]
+        asked = asked + rq[s, 8:9, :]
     asked_col = jnp.transpose(jnp.broadcast_to(asked[0:1, :], (128, 128)))
-    at_asked = jnp.where(asked_col == r * 64 + 1 + iota((128, 128), 1), 1.0, 0.0).astype(F32)[:, 0:64]
-    found = hdot(at_asked, gas_rows)
+    at_asked = jnp.where(asked_col[:, 0:1] == r * 64 + 1 + jnp.bitwise_and(iota((128, 192), 1), 63), 1.0, 0.0)
+    found = pick(at_asked, gas3)
     for s in range(nr):
         index = rq[s, 0:8, :]
         for c in range(3):
@@ -275,11 +330,8 @@
         c = to(rps.at[dst], rp.at[r], rp_s.at[k], rp_r.at[k], rad=dst)
         c.start()
         replies.append(c)
-    shares = []
-    for k in range(1, nr):
-        c = to(pres, slab.at[r], pr_s.at[k], pr_r.at[k], rad=lax.rem(r + k, nr))
-        c.start()
-        shares.append(c)
+    deposits = spread_out(sds, sd, sd_s, sd_r)
+    share_again = pass_on(shares, slab, pr_s, pr_r)
 
     loads[9].wait()
     loads[10].wait()
@@ -290,11 +342,6 @@
     for k in range(4):
         keys[k] = jnp.transpose(jnp.broadcast_to(rows8[4 + k : 5 + k, :], (128, 128)))[0:64, :]
 
-    loads[3].wait()
-    size = psv[...]
-    factor = jnp.exp(-0.5 / (size * size))
-    mass = size * size * size
-    loads[4].wait()
     for i in (5, 6, 7):
         loads[i].wait()
     rows8[0:2, 0:64] = sav[0, 0]
@@ -306,14 +353,14 @@
     live_ax = lane8 < jnp.where(low8, counts[0], counts[1] + 64)
     live_rad = lane8 < jnp.where(low8, counts[2], counts[3] + 64)
 
-    w_lo = jnp.where((col_away > 0) & (col_rank < 8) & (jnp.right_shift(col_id, 6) * 8 + col_rank == lane32), 1.0, 0.0)
-    w_hi = jnp.where((col_away > 0) & (col_rank >= 8) & (jnp.right_shift(col_id, 6) * 8 + col_rank - 8 == lane32), 1.0, 0.0)
-    w = jnp.concatenate([w_lo, w_hi], axis=0).astype(F32)[:, 0:64]
+    seat = jnp.where(col_away > 0, jnp.right_shift(col_id, 6) * 8 + jnp.bitwise_and(col_rank, 7), -1)
+    seat = jnp.concatenate([jnp.where(col_rank < 8, seat, -1), jnp.where(col_rank < 8, -1, seat)], axis=0)
+    w = jnp.where(seat[:, 0:1] == jnp.bitwise_and(iota((64, 192), 1), 63), 1.0, 0.0)
 
     for c in replies:
         c.wait_recv()
     answer = jnp.concatenate([rp[:, c].reshape(nr * 8, 128) for c in range(3)], axis=1)
-    spread = hdot(w, answer)
+    spread = pick(w, pieces(answer))
     u = []
     for c in range(3):
         lo, hi = spread[0:32, 128 * c : 128 * c + 128], spread[32:64, 128 * c : 128 * c + 128]
@@ -325,7 +372,6 @@
     cross_rad = jnp.zeros((8, 128), F32)
     tile_ax, lane_ax = jnp.right_shift(list_ax, 7), jnp.bitwise_and(list_ax, 127)
     tile_rad, lane_rad = jnp.right_shift(list_rad, 7), jnp.bitwise_and(list_rad, 127)
-    is_vel = (sub8 >= 3) & (sub8 < 6)
     for t in range(16):
         row = lambda x: jnp.broadcast_to(x[t : t + 1, :], (8, 128))
         old = jnp.concatenate([pmv[:, 128 * t : 128 * t + 128], jnp.zeros((2, 128), F32)], axis=0)
@@ -334,8 +380,6 @@
         pos = old + 0.5 * pltpu.roll(vel, 5, axis=0)
         new = jnp.where(sub8 < 3, pos, jnp.where(is_vel, vel, row(size)))
         motv[:, 128 * t : 128 * t + 128] = new[0:6]
-        m = row(mass)
-        state[:, 128 * t : 128 * t + 128] = jnp.where(is_vel, -m * (vel - old), jnp.where(sub8 == 6, m, 0.0))
         cross_ax = jnp.where(tile_ax == t, lane_gather(new, lane_ax), cross_ax)
         cross_rad = jnp.where(tile_rad == t, lane_gather(new, lane_rad), cross_rad)
     cross_ax = jnp.where(live_ax, cross_ax, 0.0)
@@ -358,35 +402,10 @@
         def _(i=i):
             crossing(i).start()
 
-    out_motion = pltpu.make_async_copy(motv, motion_o, osem.at[0])
-    out_motion.start()
-
-    sub128 = iota((128, 128), 0)
-    for t in range(16):
-        d = state[:, 128 * t : 128 * t + 128]
-        both = jnp.concatenate([jnp.where(low8, d, 0.0), jnp.where(low8, 0.0, d)], axis=0)
-        cells = jnp.where(
-            jnp.broadcast_to(offsets[t : t + 1, :], (128, 128)) == sub128, 1.0, 0.0
-        ).astype(BF16)
-        sums = lax.dot_general(
-            jnp.concatenate(split3(both), axis=0), cells, NT_DIMS, preferred_element_type=F32
-        )
-        sums = sums[0:16] + sums[16:32] + sums[32:48]
-        dp[t] = sums[0:8]
-        dp[16 + t] = sums[8:16]
-    by_comp = jnp.concatenate([dp[:, 3 + c, :] for c in range(4)], axis=1)
-    slotted = hdot(to_slot, by_comp)
-    for c in range(4):
-        sds[c] = slotted[:, 128 * c : 128 * c + 128]
-    deposits = []
-    for k in range(1, nr):
-        c = to(sds, sd.at[r], sd_s.at[k], sd_r.at[k], rad=lax.rem(r + k, nr))
-        c.start()
-        deposits.append(c)
-
     loads[8].wait()
     loads[11].wait()
-    for c in shares:
+    deposit_again = pass_on(deposits, sd, sd_s, sd_r)
+    for c in shares[:1] + share_again:
         c.wait_recv()
     slab_rows = jnp.concatenate(
         [slab[:, :, 128 * q : 128 * q + 128].reshape(nr * 16, 128) for q in range(4)], axis=0
@@ -412,23 +431,22 @@
 
     lax.fori_loop(0, 8, kind_step, 0)
 
-    for c in deposits:
+    for c in deposits[:1] + deposit_again:
         c.wait_recv()
-    row_id = jnp.broadcast_to(jnp.where(valid, ident, -1)[0:1, :], (64, 128))
-    sub64 = iota((64, 128), 0)
-    hits_own = jnp.where(row_id == r * 64 + sub64, 1.0, 0.0).astype(F32)[:, 0:32]
-    hits_far = jnp.where(jnp.broadcast_to(asked[0:1, :], (64, 128)) == r * 64 + 1 + sub64, 1.0, 0.0).astype(F32)
-    far = jnp.concatenate([sd[:, c].reshape(nr * SLOTS, 128) for c in range(4)], axis=1)
-    sources = hdot(hits_own, by_comp) + hdot(hits_far, far)
+    own_at = jnp.broadcast_to(thrice(ident)[0:1, 0:96], (64, 96))
+    far_at = jnp.broadcast_to(jnp.concatenate([asked] * 3, axis=1), (64, 384))
+    hits_own = jnp.where(own_at == r * 64 + iota((64, 96), 0), 1.0, 0.0)
+    hits_far = jnp.where(far_at == r * 64 + 1 + iota((64, 384), 0), 1.0, 0.0)
+    far = jnp.concatenate([sd[:, c].reshape(nr * SLOTS, 128) for c in range(ROWS)], axis=1)
+    sources = pick(hits_own, own3) + pick(hits_far, pieces(far))
     for q in range(4):
         rows = slice(16 * q, 16 * q + 16)
         lanes = slice(128 * q, 128 * q + 128)
+        weight = sources[rows, 0:128]
         for c in range(3):
-            gasov[c, :, lanes] = gasv[c, :, lanes] + sources[rows, 128 * c : 128 * c + 128]
-        liqv[:, lanes] = sources[rows, 384:512]
-    outs = [pltpu.make_async_copy(gasov, gas_o, osem.at[1]), pltpu.make_async_copy(liqv, liq_o, osem.at[2])]
-    for c in outs:
-        c.start()
+            g = gasv[c, :, lanes]
+            gasov[c, :, lanes] = g + (sources[rows, 128 * c + 128 : 128 * c + 256] - g * weight)
+        liqv[:, lanes] = sources[rows, 512:640]
 
     @pl.when(has_prev)
     def _():
@@ -445,8 +463,6 @@
     for q in range(4):
         lanes = slice(128 * q, 128 * q + 128)
         pimv[:, lanes] = image[:, lanes] + coup[pl.ds(q, 16, stride=4), :]
-    outs.append(pltpu.make_async_copy(pimv, pim_o, osem.at[3]))
-    outs[-1].start()
 
     for i in range(4):
 
@@ -458,12 +474,7 @@
         for f in range(7):
             arrav[0, 0, f, i : i + 1, :] = xa[i, f : f + 1, 0:64]
             arrrv[0, 0, f, i : i + 1, :] = xr[i, f : f + 1, 0:32]
-    outs.append(pltpu.make_async_copy(arrav, arra_o, osem.at[4]))
-    outs.append(pltpu.make_async_copy(arrrv, arrr_o, osem.at[5]))
-    outs[-2].start()
-    outs[-1].start()
-
-    for c in requests + replies + shares + deposits:
+    for c in requests + replies + shares + deposits + share_again + deposit_again:
         c.wait_send()
 
     @pl.when(has_next)
@@ -479,10 +490,6 @@
         @pl.when(sends_to[i])
         def _(i=i):
             crossing(i).wait_send()
-
-    out_motion.wait()
-    for c in outs:
-        c.wait()
 
 
 def out_kernel(*refs):
@@ -524,11 +531,10 @@
         V((16, 128), I32),
         V((nr, 3, 8, 128), F32),
         V((nr, 3, 8, 128), F32),
-        V((8, 2048), F32),
         V((3, 16, 128), F32),
         V((32, 8, 128), F32),
-        V((nr, 4, SLOTS, 128), F32),
-        V((4, SLOTS, 128), F32),
+        V((nr, ROWS, SLOTS, 128), F32),
+        V((ROWS, SLOTS, 128), F32),
         V((2, 8, 512), F32),
         V((4, 8, 128), F32),
         V((2, 8, 128), F32),
@@ -536,14 +542,7 @@
         V((4, 64, 128), I32),
         V((64, 128), F32),
         V((512, 384), BF16),
-        V((6, 2048), F32),
-        V((1, 1, 7, 2, 64), F32),
-        V((1, 1, 7, 2, 32), F32),
-        V((3, 16, 512), F32),
-        V((16, 512), F32),
-        V((16, 512), F32),
         dma((12,)),
-        dma((6,)),
         dma((8,)),
         dma((8,)),
         dma((8,)),
@@ -559,9 +558,9 @@
     ]
     parts = pl.pallas_call(
         functools.partial(step_kernel, na, nr),
-        out_shape=outs,
+        out_shape=[pltpu.VMEM(o.shape, o.dtype) for o in outs],
         in_specs=[anyspec] * 12,
-        out_specs=[anyspec] * 6,
+        out_specs=[pl.BlockSpec(memory_space=pltpu.VMEM)] * 6,
         scratch_shapes=scratch,
         compiler_params=pltpu.CompilerParams(
             collective_id=0, has_side_effects=True, vmem_limit_bytes=VMEM_BYTES
@@ -584,10 +583,10 @@
     motion, axial, radial, gas_out, load, image = pl.pallas_call(
         out_kernel,
         out_shape=outs,
-        in_specs=[anyspec] * 6,
+        in_specs=[pl.BlockSpec(memory_space=pltpu.VMEM)] * 6,
         out_specs=[anyspec] * 6,
         scratch_shapes=[dma((6,))],
-        compiler_params=pltpu.CompilerParams(vmem_limit_bytes=VMEM_BYTES),
+        compiler_params=pltpu.CompilerParams(vmem_limit_bytes=1024 * 1024),
         name="copy_out",
     )(*parts)
     return motion, jnp.swapaxes(axial, 2, 3), jnp.swapaxes(radial, 2, 3), gas_out, load, image

time: 40.1 us -> 26.4 us (0.66)
  the two profiles are of different devices: /device:TPU:393 before, /device:TPU:448 now
where the time goes in v2:
time: 26.4 us; the launch traced here: 26.3 us
  Pallas kernels  25.7 us (97%)
  between operations  0.64 us (2%)
    pallas_call x1, Pallas kernels, on_device(): pl.pallas_call(functools.partial(step_kernel, na, nr), out_shape=[pltpu.V...  24.9 us
    pallas_call x1, Pallas kernels, on_device(): pl.pallas_call(out_kernel, out_shape=outs, in_specs=[pl.BlockSpec(memory_...  0.74 us

profile of v2, /device:TPU:448, one launch (start us, length us, event | category | flops | bytes accessed | tf_op | source)
XLA Modules:
  0.0 26.3 jit_solution(11846691586985083803)
XLA Ops:
  0.6 24.9 %step.1 = (f32[6,2048]{1,0:T(8,128)S(1)}, f32[1,1,7,2,64]{4,3,2,1,0:T(2,128)S(1)}, f32[1,1,7,2,32]{4,3,2,1,0:T(2,128)S(1)}, f32[3,16,512]{2,1,0:T(8,128)S(1)}, f...) custom-call(f32[6,2048]{1,0:T(8,128)} %pm.1, f32[16,128]{1,0:T(8,128)} %bitcast.7, s32[1,32]{1,0:T(1,128)} %bitcast.11, ...), custom_call_target="tpu_custom_call" | custom-call | tf_op jit(solution)/shard_map/step/pallas_call | solution.py:559
  25.6 0.7 %copy_out.1 = (f32[6,2048]{1,0:T(8,128)}, f32[1,1,7,2,64]{4,3,2,1,0:T(2,128)}, f32[1,1,7,2,32]{4,3,2,1,0:T(2,128)}, f32[3,16,512]{2,1,0:T(8,128)}, f32[16,512]{1,0:T(8,128)}, /*index=5*/f32[16,512]{1,0:T(8,128)}) custom-call(f32[6,2048]{1,0:T(8,128)S(1)} %get-tuple-element.18.refs_0_, f32[1,1,7,2,64]{4,3,2,1,0:T(2,128)S(1)} %get-tuple-element.19.refs_1_, ...), custom_call_target="tpu_custom_call" | custom-call | tf_op jit(solution)/shard_map/copy_out/pallas_call | solution.py:583

commit v3 on v2

--- a/solution.py
+++ b/solution.py
@@ -95,6 +95,8 @@
     keys,
     coup,
     p3,
+    chosen,
+    tab3,
     lsem,
     rq_s,
     rq_r,
@@ -108,6 +110,8 @@
     ha_r,
     x_s,
     x_r,
+    slab_go,
+    ax_go,
 ):
     a = lax.axis_index("ax")
     r = lax.axis_index("rad")
@@ -119,17 +123,24 @@
             src_ref=src, dst_ref=dst, send_sem=ssem, recv_sem=rsem, device_id=where, device_id_type=MESH
         )
 
+    core = lax.rem(r, 2)
+    sibling = r + 1 - 2 * core
     barrier = pltpu.get_barrier_semaphore()
-    for k in range(1, nr):
-        pl.semaphore_signal(barrier, inc=1, device_id={"rad": lax.rem(r + k, nr)}, device_id_type=MESH)
+    for k in range(1, 4):
+        even = lax.rem(r - core + 2 * k, nr)
+        pl.semaphore_signal(barrier, inc=1, device_id={"rad": even}, device_id_type=MESH)
+
+    @pl.when(core == 1)
+    def _():
+        pl.semaphore_signal(barrier, inc=1, device_id={"rad": sibling}, device_id_type=MESH)
 
     @pl.when(has_prev)
     def _():
-        pl.semaphore_signal(barrier, inc=1, device_id={"ax": a - 1}, device_id_type=MESH)
+        pl.semaphore_signal(barrier, inc=1, device_id={"ax": a - 1, "rad": r - core + 1}, device_id_type=MESH)
 
     @pl.when(has_next)
     def _():
-        pl.semaphore_signal(barrier, inc=1, device_id={"ax": a + 1}, device_id_type=MESH)
+        pl.semaphore_signal(barrier, inc=1, device_id={"ax": a + 1, "rad": r - core + 1}, device_id_type=MESH)
 
     loads = [
         pltpu.make_async_copy(src, dst, lsem.at[i])
@@ -225,10 +236,14 @@
     def _():
         xr[1] = jnp.zeros((8, 128), F32)
 
-    pl.semaphore_wait(barrier, nr - 1 + has_prev.astype(I32) + has_next.astype(I32))
-
-    core = lax.rem(r, 2)
-    sibling = r + 1 - 2 * core
+    @pl.when(core == 0)
+    def _():
+        pl.semaphore_wait(barrier, nr - 1)
+        pl.semaphore_signal(slab_go, inc=1, device_id={"rad": sibling}, device_id_type=MESH)
+
+    @pl.when(core == 1)
+    def _():
+        pl.semaphore_wait(slab_go, 1)
 
     def spread_out(src, dst, ssem, rsem):
         copies = []
@@ -262,14 +277,6 @@
 
     def halo_prev():
         return to(pres.at[0:8], halo.at[1], ha_s.at[1], ha_r.at[1], ax=a - 1)
-
-    @pl.when(has_next)
-    def _():
-        halo_next().start()
-
-    @pl.when(has_prev)
-    def _():
-        halo_prev().start()
 
     loads[2].wait()
     gas_rows = jnp.concatenate(
@@ -286,6 +293,25 @@
         part = found[:, 128 * c : 128 * c + 128]
         uown[c] = jnp.where(low16, lane_gather(part[0:16], offsets), lane_gather(part[16:32], offsets))
 
+    for c in requests:
+        c.wait_recv()
+    asked = rq[0, 8:9, :]
+    for s in range(1, nr):
+        asked = asked + rq[s, 8:9, :]
+    asked_col = jnp.transpose(jnp.broadcast_to(asked[0:1, :], (128, 128)))
+    at_asked = jnp.where(asked_col[:, 0:1] == r * 64 + 1 + jnp.bitwise_and(iota((128, 192), 1), 63), 1.0, 0.0)
+    found = pick(at_asked, gas3)
+    for s in range(nr):
+        index = rq[s, 0:8, :]
+        for c in range(3):
+            part = found[SLOTS * s : SLOTS * s + 16, 128 * c : 128 * c + 128]
+            rps[s, c] = jnp.where(low8, lane_gather(part[0:8], index), lane_gather(part[8:16], index))
+    replies = []
+    for k in range(1, nr):
+        dst = lax.rem(r + k, nr)
+        c = to(rps.at[dst], rp.at[r], rp_s.at[k], rp_r.at[k], rad=dst)
+        c.start()
+        replies.append(c)
     loads[3].wait()
     size = psv[...]
     factor = jnp.exp(-0.5 / (size * size))
@@ -311,25 +337,6 @@
     for c in range(ROWS):
         sds[c] = slotted[:, 128 * c : 128 * c + 128]
 
-    for c in requests:
-        c.wait_recv()
-    asked = rq[0, 8:9, :]
-    for s in range(1, nr):
-        asked = asked + rq[s, 8:9, :]
-    asked_col = jnp.transpose(jnp.broadcast_to(asked[0:1, :], (128, 128)))
-    at_asked = jnp.where(asked_col[:, 0:1] == r * 64 + 1 + jnp.bitwise_and(iota((128, 192), 1), 63), 1.0, 0.0)
-    found = pick(at_asked, gas3)
-    for s in range(nr):
-        index = rq[s, 0:8, :]
-        for c in range(3):
-            part = found[SLOTS * s : SLOTS * s + 16, 128 * c : 128 * c + 128]
-            rps[s, c] = jnp.where(low8, lane_gather(part[0:8], index), lane_gather(part[8:16], index))
-    replies = []
-    for k in range(1, nr):
-        dst = lax.rem(r + k, nr)
-        c = to(rps.at[dst], rp.at[r], rp_s.at[k], rp_r.at[k], rad=dst)
-        c.start()
-        replies.append(c)
     deposits = spread_out(sds, sd, sd_s, sd_r)
     share_again = pass_on(shares, slab, pr_s, pr_r)
 
@@ -341,6 +348,25 @@
     rows8[4:8, 0:64] = key
     for k in range(4):
         keys[k] = jnp.transpose(jnp.broadcast_to(rows8[4 + k : 5 + k, :], (128, 128)))[0:64, :]
+    lane64 = iota((64, 128), 1)
+
+    def choose(t, carry):
+        for q in range(4):
+            want = t * 512 + q * 128 + lane64
+            g = jnp.where(keys[0] == want, 1.0, 0.0)
+            for k in range(1, 4):
+                g = g + jnp.where(keys[k] == want, 1.0, 0.0)
+            chosen[pl.ds(pl.multiple_of(64 * t, 64), 64), 128 * q : 128 * q + 128] = g.astype(BF16)
+        return carry
+
+    lax.fori_loop(0, 8, choose, 0)
+    loads[11].wait()
+    for t in range(8):
+        tab = tabv[t]
+        tab_high = tab.astype(BF16)
+        tab3[:, 128 * t : 128 * t + 128] = tab_high
+        tab3[:, 1024 + 128 * t : 1152 + 128 * t] = tab_high
+        tab3[:, 2048 + 128 * t : 2176 + 128 * t] = (tab - tab_high.astype(F32)).astype(BF16)
 
     for i in (5, 6, 7):
         loads[i].wait()
@@ -394,6 +420,15 @@
         where = ({"ax": a + 1}, {"ax": a - 1}, {"rad": r + 1}, {"rad": r - 1})[i]
         return to(xs.at[i], dst, x_s.at[i], x_r.at[i], **where)
 
+    @pl.when(core == 1)
+    def _():
+        pl.semaphore_wait(barrier, 2 * (has_prev.astype(I32) + has_next.astype(I32)))
+        pl.semaphore_signal(ax_go, inc=1, device_id={"rad": sibling}, device_id_type=MESH)
+
+    @pl.when(core == 0)
+    def _():
+        pl.semaphore_wait(ax_go, 1)
+
     sends_to = (has_next, has_prev, has_out, has_in)
     comes_from = (has_prev, has_next, has_in, has_out)
     for i in range(4):
@@ -402,34 +437,32 @@
         def _(i=i):
             crossing(i).start()
 
+    @pl.when(has_next)
+    def _():
+        halo_next().start()
+
+    @pl.when(has_prev)
+    def _():
+        halo_prev().start()
+
     loads[8].wait()
-    loads[11].wait()
-    deposit_again = pass_on(deposits, sd, sd_s, sd_r)
     for c in shares[:1] + share_again:
         c.wait_recv()
     slab_rows = jnp.concatenate(
         [slab[:, :, 128 * q : 128 * q + 128].reshape(nr * 16, 128) for q in range(4)], axis=0
     )
     p3[...] = jnp.concatenate(split3(slab_rows), axis=1)
-    coup[...] = jnp.zeros((64, 128), F32)
-    lane64 = iota((64, 128), 1)
-
-    def kind_step(t, carry):
-        chosen = []
-        for q in range(4):
-            want = t * 512 + q * 128 + lane64
-            g = jnp.where(keys[0] == want, 1.0, 0.0)
-            for k in range(1, 4):
-                g = g + jnp.where(keys[k] == want, 1.0, 0.0)
-            chosen.append(g.astype(BF16))
-        three = jnp.dot(jnp.concatenate(chosen, axis=1), p3[...], preferred_element_type=F32)
-        grouped = three[:, 0:128] + three[:, 128:256] + three[:, 256:384]
-        coup[...] += lax.dot_general(
-            grouped, tabv[t], NT_DIMS, precision=HIGHEST, preferred_element_type=F32
-        )
-        return carry
-
-    lax.fori_loop(0, 8, kind_step, 0)
+    three = jnp.dot(chosen[...], p3[...], preferred_element_type=F32)
+    grouped = three[:, 0:128] + three[:, 128:256] + three[:, 256:384]
+    high = grouped.astype(BF16)
+    low = (grouped - high.astype(F32)).astype(BF16)
+    high = jnp.concatenate([high[64 * t : 64 * t + 64] for t in range(8)], axis=1)
+    low = jnp.concatenate([low[64 * t : 64 * t + 64] for t in range(8)], axis=1)
+    coup[...] = lax.dot_general(
+        jnp.concatenate([high, low, high], axis=1), tab3[...], NT_DIMS, preferred_element_type=F32
+    )
+
+    deposit_again = pass_on(deposits, sd, sd_s, sd_r)
 
     for c in deposits[:1] + deposit_again:
         c.wait_recv()
@@ -542,6 +575,8 @@
         V((4, 64, 128), I32),
         V((64, 128), F32),
         V((512, 384), BF16),
+        V((512, 512), BF16),
+        V((128, 3072), BF16),
         dma((12,)),
         dma((8,)),
         dma((8,)),
@@ -555,6 +590,8 @@
         dma((2,)),
         dma((4,)),
         dma((4,)),
+        pltpu.SemaphoreType.REGULAR,
+        pltpu.SemaphoreType.REGULAR,
     ]
     parts = pl.pallas_call(
         functools.partial(step_kernel, na, nr),

time: 26.4 us -> 24.7 us (0.936)
  the two profiles are of different devices: /device:TPU:448 before, /device:TPU:328 now
where the time goes in v3:
time: 24.7 us; the launch traced here: 24.5 us
  Pallas kernels  23.9 us (97%)
  between operations  0.64 us (3%)
    pallas_call x1, Pallas kernels, on_device(): pl.pallas_call(functools.partial(step_kernel, na, nr), out_shape=[pltpu.V...  23.1 us
    pallas_call x1, Pallas kernels, on_device(): pl.pallas_call(out_kernel, out_shape=outs, in_specs=[pl.BlockSpec(memory_...  0.74 us

profile of v3, /device:TPU:328, one launch (start us, length us, event | category | flops | bytes accessed | tf_op | source)
XLA Modules:
  0.0 24.5 jit_solution(1914446109801496115)
XLA Ops:
  0.6 23.1 %step.1 = (f32[6,2048]{1,0:T(8,128)S(1)}, f32[1,1,7,2,64]{4,3,2,1,0:T(2,128)S(1)}, f32[1,1,7,2,32]{4,3,2,1,0:T(2,128)S(1)}, f32[3,16,512]{2,1,0:T(8,128)S(1)}, f...) custom-call(f32[6,2048]{1,0:T(8,128)} %pm.1, f32[16,128]{1,0:T(8,128)} %bitcast.7, s32[1,32]{1,0:T(1,128)} %bitcast.11, ...), custom_call_target="tpu_custom_call" | custom-call | tf_op jit(solution)/shard_map/step/pallas_call | solution.py:596
  23.8 0.7 %copy_out.1 = (f32[6,2048]{1,0:T(8,128)}, f32[1,1,7,2,64]{4,3,2,1,0:T(2,128)}, f32[1,1,7,2,32]{4,3,2,1,0:T(2,128)}, f32[3,16,512]{2,1,0:T(8,128)}, f32[16,512]{1,0:T(8,128)}, /*index=5*/f32[16,512]{1,0:T(8,128)}) custom-call(f32[6,2048]{1,0:T(8,128)S(1)} %get-tuple-element.18.refs_0_, f32[1,1,7,2,64]{4,3,2,1,0:T(2,128)S(1)} %get-tuple-element.19.refs_1_, ...), custom_call_target="tpu_custom_call" | custom-call | tf_op jit(solution)/shard_map/copy_out/pallas_call | solution.py:620

commit v4 on v3

--- a/solution.py
+++ b/solution.py
@@ -86,8 +86,11 @@
     rps,
     uown,
     dp,
-    sd,
-    sds,
+    raw,
+    raw_out,
+    vt,
+    st,
+    df,
     halo,
     xs,
     xa,
@@ -216,7 +219,7 @@
 
     rq[r] = jnp.zeros((16, 128), I32)
     rp[r] = jnp.zeros((3, 8, 128), F32)
-    sd[r] = jnp.zeros((ROWS, SLOTS, 128), F32)
+    raw[r] = jnp.zeros((4, 8, 128), F32)
 
     @pl.when(jnp.logical_not(has_prev))
     def _():
@@ -270,13 +273,28 @@
         c.start()
         requests.append(c)
 
-    shares = spread_out(pres, slab, pr_s, pr_r)
 
     def halo_next():
         return to(pres.at[8:16], halo.at[0], ha_s.at[0], ha_r.at[0], ax=a + 1)
 
     def halo_prev():
         return to(pres.at[0:8], halo.at[1], ha_s.at[1], ha_r.at[1], ax=a - 1)
+
+    loads[3].wait()
+    size = psv[...]
+    loads[4].wait()
+    for t in range(16):
+        vt[:, t, :] = pmv[3:6, 128 * t : 128 * t + 128]
+    flat = jnp.concatenate([vt[0], vt[1], vt[2], size], axis=1)
+    turned = [pltpu.roll(x, 64, axis=1) for x in (vt[0], vt[1], vt[2], size)]
+    flat = pieces(jnp.concatenate([flat, jnp.concatenate(turned, axis=1)], axis=0))
+    slot_of = jnp.broadcast_to(thrice(row_rank)[0:1, 0:96], (SLOTS, 96))
+    flat = pick(jnp.where(slot_of == iota((SLOTS, 96), 0), 1.0, 0.0), flat)
+    for c in range(4):
+        part = flat[:, 128 * c : 128 * c + 128]
+        raw_out[c] = jnp.where(low8, part[0:8], pltpu.roll(part[8:16], 64, axis=1))
+    raws = spread_out(raw_out, raw, sd_s, sd_r)
+    shares = spread_out(pres, slab, pr_s, pr_r)
 
     loads[2].wait()
     gas_rows = jnp.concatenate(
@@ -312,12 +330,9 @@
         c = to(rps.at[dst], rp.at[r], rp_s.at[k], rp_r.at[k], rad=dst)
         c.start()
         replies.append(c)
-    loads[3].wait()
-    size = psv[...]
     factor = jnp.exp(-0.5 / (size * size))
     mass = size * size * size
     share = mass * (1.0 - factor)
-    loads[4].wait()
     is_vel = (sub8 >= 3) & (sub8 < 6)
     sub128 = iota((128, 128), 0)
     for t in range(16):
@@ -332,12 +347,8 @@
         dp[t] = sums[0:8]
         dp[16 + t] = sums[8:16]
     own3 = pieces(jnp.concatenate([dp[:, 2 + c, :] for c in range(ROWS)], axis=1))
-    slot_of = jnp.broadcast_to(thrice(row_rank)[0:1, 0:96], (SLOTS, 96))
-    slotted = pick(jnp.where(slot_of == iota((SLOTS, 96), 0), 1.0, 0.0), own3)
-    for c in range(ROWS):
-        sds[c] = slotted[:, 128 * c : 128 * c + 128]
-
-    deposits = spread_out(sds, sd, sd_s, sd_r)
+
+    raw_again = pass_on(raws, raw, sd_s, sd_r)
     share_again = pass_on(shares, slab, pr_s, pr_r)
 
     loads[9].wait()
@@ -445,6 +456,30 @@
     def _():
         halo_prev().start()
 
+    for c in raws[:1] + raw_again:
+        c.wait_recv()
+    blank = jnp.zeros((8, 128), F32)
+    df[pl.ds(pl.multiple_of(SLOTS * r, SLOTS), SLOTS)] = jnp.zeros((SLOTS, 8, 128), F32)
+    for k in range(1, nr):
+        s = lax.rem(r + k, nr)
+        d = raw[s, 3]
+        m = d * d * d
+        k_ = m * (1.0 - jnp.exp(-0.5 / (d * d)))
+        values = [k_, k_ * raw[s, 0], k_ * raw[s, 1], k_ * raw[s, 2], m]
+        for c in range(8):
+            value = values[c] if c < ROWS else blank
+            hi = value.astype(BF16).astype(F32) if c < ROWS else blank
+            lo = value - hi if c < ROWS else blank
+            for i, piece in enumerate((hi, lo)):
+                st[k, 16 * i + c] = jnp.where(low8, piece, 0.0) if c < ROWS else blank
+                st[k, 16 * i + 8 + c] = jnp.where(low8, 0.0, piece) if c < ROWS else blank
+        for i in range(8):
+            cells = jnp.where(jnp.broadcast_to(rq[s, i : i + 1, :], (128, 128)) == sub128, 1.0, 0.0).astype(BF16)
+            sums = lax.dot_general(st[k, :, i, :].astype(BF16), cells, NT_DIMS, preferred_element_type=F32)
+            sums = sums[0:16] + sums[16:32]
+            df[SLOTS * s + i] = sums[0:8]
+            df[SLOTS * s + 8 + i] = sums[8:16]
+
     loads[8].wait()
     for c in shares[:1] + share_again:
         c.wait_recv()
@@ -462,15 +497,11 @@
         jnp.concatenate([high, low, high], axis=1), tab3[...], NT_DIMS, preferred_element_type=F32
     )
 
-    deposit_again = pass_on(deposits, sd, sd_s, sd_r)
-
-    for c in deposits[:1] + deposit_again:
-        c.wait_recv()
     own_at = jnp.broadcast_to(thrice(ident)[0:1, 0:96], (64, 96))
     far_at = jnp.broadcast_to(jnp.concatenate([asked] * 3, axis=1), (64, 384))
     hits_own = jnp.where(own_at == r * 64 + iota((64, 96), 0), 1.0, 0.0)
     hits_far = jnp.where(far_at == r * 64 + 1 + iota((64, 384), 0), 1.0, 0.0)
-    far = jnp.concatenate([sd[:, c].reshape(nr * SLOTS, 128) for c in range(ROWS)], axis=1)
+    far = jnp.concatenate([df[:, c, :] for c in range(ROWS)], axis=1)
     sources = pick(hits_own, own3) + pick(hits_far, pieces(far))
     for q in range(4):
         rows = slice(16 * q, 16 * q + 16)
@@ -507,7 +538,7 @@
         for f in range(7):
             arrav[0, 0, f, i : i + 1, :] = xa[i, f : f + 1, 0:64]
             arrrv[0, 0, f, i : i + 1, :] = xr[i, f : f + 1, 0:32]
-    for c in requests + replies + shares + deposits + share_again + deposit_again:
+    for c in requests + replies + shares + raws + share_again + raw_again:
         c.wait_send()
 
     @pl.when(has_next)
@@ -566,8 +597,11 @@
         V((nr, 3, 8, 128), F32),
         V((3, 16, 128), F32),
         V((32, 8, 128), F32),
-        V((nr, ROWS, SLOTS, 128), F32),
-        V((ROWS, SLOTS, 128), F32),
+        V((nr, 4, 8, 128), F32),
+        V((4, 8, 128), F32),
+        V((3, 16, 128), F32),
+        V((nr, 32, 8, 128), F32),
+        V((nr * SLOTS, 8, 128), F32),
         V((2, 8, 512), F32),
         V((4, 8, 128), F32),
         V((2, 8, 128), F32),

time: 24.7 us -> 24.4 us (0.988)
  the two profiles are of different devices: /device:TPU:328 before, /device:TPU:448 now
where the time goes in v4:
time: 24.4 us; the launch traced here: 24.3 us
  Pallas kernels  23.6 us (97%)
  between operations  0.64 us (3%)
    pallas_call x1, Pallas kernels, on_device(): pl.pallas_call(functools.partial(step_kernel, na, nr), out_shape=[pltpu.V...  22.9 us
    pallas_call x1, Pallas kernels, on_device(): pl.pallas_call(out_kernel, out_shape=outs, in_specs=[pl.BlockSpec(memory_...  0.74 us

profile of v4, /device:TPU:448, one launch (start us, length us, event | category | flops | bytes accessed | tf_op | source)
XLA Modules:
  0.0 24.3 jit_solution(4107458047245068727)
XLA Ops:
  0.6 22.9 %step.1 = (f32[6,2048]{1,0:T(8,128)S(1)}, f32[1,1,7,2,64]{4,3,2,1,0:T(2,128)S(1)}, f32[1,1,7,2,32]{4,3,2,1,0:T(2,128)S(1)}, f32[3,16,512]{2,1,0:T(8,128)S(1)}, f...) custom-call(f32[6,2048]{1,0:T(8,128)} %pm.1, f32[16,128]{1,0:T(8,128)} %bitcast.7, s32[1,32]{1,0:T(1,128)} %bitcast.11, ...), custom_call_target="tpu_custom_call" | custom-call | tf_op jit(solution)/shard_map/step/pallas_call | solution.py:630
  23.5 0.7 %copy_out.1 = (f32[6,2048]{1,0:T(8,128)}, f32[1,1,7,2,64]{4,3,2,1,0:T(2,128)}, f32[1,1,7,2,32]{4,3,2,1,0:T(2,128)}, f32[3,16,512]{2,1,0:T(8,128)}, f32[16,512]{1,0:T(8,128)}, /*index=5*/f32[16,512]{1,0:T(8,128)}) custom-call(f32[6,2048]{1,0:T(8,128)S(1)} %get-tuple-element.18.refs_0_, f32[1,1,7,2,64]{4,3,2,1,0:T(2,128)S(1)} %get-tuple-element.19.refs_1_, ...), custom_call_target="tpu_custom_call" | custom-call | tf_op jit(solution)/shard_map/copy_out/pallas_call | solution.py:654
